TPU v7x, 256 devices: a whole 4x4x8 slice. The times are simulated.
256 devices in a mesh: blk: 32 (over y_hi, z, core), lag: 8 (over y_lo, x).
Axes of the slice: x: 4, y: 4 (y_hi: 2, y_lo: 2; y = y_hi * 2 + y_lo), z: 8, core: 2. Of those that a mesh axis runs over, the one named last changes fastest.
Arguments:
- spectra: bfloat16 [4096, 3, 2, 1024], P('blk', None, None, 'lag'), may hold values from -6 to 6
- band: int32 [4096, 2], P('blk'), may hold values from 0 to 1024, as said below
- pair_lists: int32 [32, 17, 96, 2], P('blk'), may hold values from 0 to 127
- pair_counts: int32 [32, 17], P('blk'), may hold values from 32 to 96, as said below
Outputs:
- gradient: float32 [4096, 3, 2, 1024], P('blk', None, None, 'lag')
Inputs may be any that keep to these rules, and one draw needn't show every extreme that they name: band[s, 0] < band[s, 1]; band[s, 0] is at most 128 and band[s, 1] at least 896; some station starts at 0 and some ends at 1024. `pair_counts`: at least a third of the slots are used; in every block one offset uses all 96 slots.
All inputs are finite; a program needn't handle non-finite values.
Results may differ from a plain program's by a relative error of at most 0.0045.
Values may be sent and summed in bfloat16 or wider, within the bound.
No kernel may reach another device: no remote copies, remote signals or barrier semaphores. Data moves between devices by JAX's collectives and lax.ppermute only.
A program may use at most 64 MiB of HBM per device.

v0:
```python
import math
import jax
import jax.numpy as jnp
from jax import lax
from jax.sharding import PartitionSpec as P


def from_behind(block, axis, distance):
    devices = range(lax.axis_size(axis))
    route = [((i - distance) % len(devices), i) for i in devices]
    return lax.ppermute(block, axis, route)


def phase_table(freq_ids, lag_ids, lag_total, freq_total):
    turns = freq_ids[:, None] * lag_ids[None, :] % lag_total
    angle = turns.astype(jnp.float32) * (2.0 * jnp.pi / lag_total)
    factor = 1.0 / jnp.sqrt(jnp.float32(freq_total))
    return jnp.stack([jnp.cos(angle) * factor, -jnp.sin(angle) * factor], 0).astype(jnp.bfloat16)


def whiten(spectra, band, freq_ids):
    values = spectra.astype(jnp.float32)
    meansq = jnp.mean(values * values, axis=(1, 2))
    inside = (freq_ids[None, :] >= band[:, 0:1]) & (freq_ids[None, :] < band[:, 1:2])
    factor = jnp.where(inside, 1.0 / jnp.sqrt(jnp.maximum(meansq, 0.25)), 0.0)
    return (values * factor[:, None, None, :]).astype(jnp.bfloat16)


def on_device(spectra, band, pair_lists, pair_counts):
    stations, comps, parts, bins_local = spectra.shape
    slots = pair_lists.shape[2]
    steps = pair_lists.shape[1]
    lanes = lax.axis_size("lag")
    freq_total = bins_local * lanes
    lag_total = 2 * freq_total
    lag_local = lag_total // lanes
    width = comps * parts * bins_local
    lane = lax.axis_index("lag")
    freq_ids = lane * bins_local + jnp.arange(bins_local, dtype=jnp.int32)
    lag_ids = lane * lag_local + jnp.arange(lag_local, dtype=jnp.int32)
    resident = whiten(spectra, band, freq_ids)
    local_table = phase_table(
        freq_ids, jnp.arange(lag_total, dtype=jnp.int32), lag_total, freq_total
    )
    weight = 1.0 + 3.0 * lag_ids.astype(jnp.float32) / lag_total
    station_ids = jnp.arange(stations, dtype=jnp.int32)
    slot_ids = jnp.arange(slots, dtype=jnp.int32)

    def forward(cross):
        return lax.psum_scatter(
            jnp.einsum("prf,rft->tp", cross, local_table, preferred_element_type=jnp.float32),
            "lag",
            scatter_dimension=0,
            tiled=True,
        ).T

    def back(piece):
        return jnp.einsum("pt,rft->prf", piece, local_table, preferred_element_type=jnp.float32)

    def correlate(arriving, pairs, count):
        first = pairs[:, 0]
        second = pairs[:, 1]
        pick_first = (first[:, None] == station_ids[None, :]).astype(jnp.bfloat16)
        pick_second = (second[:, None] == station_ids[None, :]).astype(jnp.bfloat16)
        rows_a = jnp.dot(
            pick_first, resident.reshape(stations, width), preferred_element_type=jnp.float32
        )
        rows_b = jnp.dot(
            pick_second, arriving.reshape(stations, width), preferred_element_type=jnp.float32
        )
        rows_a = rows_a.reshape(slots, comps, parts, bins_local)
        rows_b = rows_b.reshape(slots, comps, parts, bins_local)
        real_a, imag_a = (rows_a[:, :, 0], rows_a[:, :, 1])
        real_b, imag_b = (rows_b[:, :, 0], rows_b[:, :, 1])
        valid = (slot_ids < count).astype(jnp.float32)[:, None]
        cross_real = jnp.sum(real_a * real_b + imag_a * imag_b, axis=1) * valid
        cross_imag = jnp.sum(imag_a * real_b - real_a * imag_b, axis=1) * valid
        cross = jnp.stack([cross_real, cross_imag], 1).astype(jnp.bfloat16)
        lagged = forward(cross)
        energy = lax.psum(jnp.sum(weight[None, :] * lagged * lagged, axis=1) / lag_total, "lag")
        adjoint = (weight[None, :] * lagged / jnp.sqrt(energy + 1e-05)[:, None]).astype(
            jnp.bfloat16
        )
        spectral = back(lax.all_gather(adjoint, "lag", axis=1, tiled=True))
        adj_real = spectral[:, None, 0]
        adj_imag = spectral[:, None, 1]
        near = jnp.stack(
            [adj_real * real_b - adj_imag * imag_b, adj_real * imag_b + adj_imag * real_b], 2
        )
        far = jnp.stack(
            [adj_real * real_a + adj_imag * imag_a, adj_real * imag_a - adj_imag * real_a], 2
        )
        near = near.astype(jnp.bfloat16).reshape(slots, width)
        far = far.astype(jnp.bfloat16).reshape(slots, width)
        own = jnp.einsum("ps,pw->sw", pick_first, near, preferred_element_type=jnp.float32)
        return (own, far, second, pick_second)

    def visit(step, arriving, total, carried):
        own, far, second, pick_second = correlate(
            arriving, pair_lists[0, step], pair_counts[0, step]
        )
        total = total + own
        carried = carried + jnp.einsum(
            "ps,pw->sw", pick_second, far, preferred_element_type=jnp.float32
        )
        return (total, carried)

    def advance(step, state):
        arriving, total, carried = state
        arriving = from_behind(arriving, "blk", 1)
        carried = from_behind(carried, "blk", 1)
        total, carried = visit(step, arriving, total, carried)
        return (arriving, total, carried)

    start_carried = jnp.zeros((stations, width), jnp.float32)
    total, carried = visit(0, resident, jnp.zeros((stations, width), jnp.float32), start_carried)
    arriving, total, carried = lax.fori_loop(1, steps, advance, (resident, total, carried))
    total = total + from_behind(carried, "blk", -(steps - 1))
    gradient = total / math.sqrt(slots)
    return gradient.reshape(stations, comps, parts, bins_local)


def solution(mesh):
    in_specs = (
        P("blk", None, None, "lag"),
        P("blk", None),
        P("blk", None, None, None),
        P("blk", None),
    )
    out_specs = P("blk", None, None, "lag")
    return jax.shard_map(
        on_device, mesh=mesh, in_specs=in_specs, out_specs=out_specs, check_vma=False
    )
```

profile of v0, /device:TPU:8, one launch (start us, length us, event | category | flops | bytes accessed | tf_op | source)
XLA Modules:
  0.0 1684.5 jit_solution(6176703667037175156)
XLA Ops:
  16.2 42.7 %reduce-scatter.3.cloned.1.call-done = f32[256,96]{0,1:T(8,128)} async-done(((f32[2048,96]{0,1:T(8,128)}), f32[256,96]{0,1:T(8,128)}) %reduce-scatter.3.cloned.1.call-update) | async-done | bytes 98320 | tf_op jit(solution)/shard_map/reduce_scatter | solution.py:50
  60.0 17.5 %psum.21 = f32[96]{0:T(128)S(1)} all-reduce(f32[96]{0:T(128)S(1)} %broadcast_multiply_fusion.1), channel_id=1, replica_groups=mesh['blk'=32,'lag'=8] {'lag'}, use_global_device_ids=true, to_apply=%region_5.6 | all-reduce | flops 96 | bytes 768 | tf_op jit(solution)/shard_map/psum | solution.py:80
  78.5 28.8 %all_gather.13 = bf16[96,2048]{1,0:T(8,128)(2,1)S(1)} all-gather(bf16[96,256]{1,0:T(8,128)(2,1)S(1)} %fusion.43), channel_id=1, replica_groups=mesh['blk'=32,'lag'=8] {'lag'}, dimensions={1}, use_global_device_ids=true | all-gather | bytes 442368 | tf_op jit(solution)/shard_map/all_gather | solution.py:84
  109.0 1558.6 %while.21 = (s32[]{:T(128)}, bf16[128,3,2,128]{0,3,2,1:T(8,128)(2,1)S(1)}, f32[128,768]{1,0:T(8,128)S(1)}, f32[128,768]{1,0:T(8,128)S(1)}, s32[1,17,96,2]{2,3,1,...) while((s32[]{:T(128)}, ...), condition=%wide.region_12.13_spmd.clone.clone, body=%wide.region_6.12_spmd.clone.clone.sunk | while | flops 278300032 | bytes 16166447 | solution.py:117
  119.6 36.8 %reduce-scatter.5.cloned.1.call-done = f32[256,96]{0,1:T(8,128)} async-done(((f32[2048,96]{0,1:T(8,128)}), f32[256,96]{0,1:T(8,128)}) %reduce-scatter.5.cloned.1.call-update) | async-done | bytes 98320 | tf_op jit(solution)/shard_map/while/body/eval_jaxpr/reduce_scatter | solution.py:50
  157.3 17.6 %psum.25 = f32[96]{0:T(128)S(1)} all-reduce(f32[96]{0:T(128)S(1)} %broadcast_multiply_fusion.3), channel_id=1, replica_groups=mesh['blk'=32,'lag'=8] {'lag'}, use_global_device_ids=true, to_apply=%region_11.11 | all-reduce | flops 96 | bytes 768 | tf_op jit(solution)/shard_map/while/body/eval_jaxpr/psum | solution.py:80
  175.9 28.8 %all_gather.17 = bf16[96,2048]{1,0:T(8,128)(2,1)S(1)} all-gather(bf16[96,256]{1,0:T(8,128)(2,1)S(1)} %fusion.96), channel_id=1, replica_groups=mesh['blk'=32,'lag'=8] {'lag'}, dimensions={1}, use_global_device_ids=true | all-gather | bytes 442368 | tf_op jit(solution)/shard_map/while/body/eval_jaxpr/all_gather | solution.py:84
  217.0 36.7 %reduce-scatter.5.cloned.1.call-done = f32[256,96]{0,1:T(8,128)} async-done(((f32[2048,96]{0,1:T(8,128)}), f32[256,96]{0,1:T(8,128)}) %reduce-scatter.5.cloned.1.call-update) | async-done | bytes 98320 | tf_op jit(solution)/shard_map/while/body/eval_jaxpr/reduce_scatter | solution.py:50
  273.2 28.8 %all_gather.17 = bf16[96,2048]{1,0:T(8,128)(2,1)S(1)} all-gather(bf16[96,256]{1,0:T(8,128)(2,1)S(1)} %fusion.96), channel_id=1, replica_groups=mesh['blk'=32,'lag'=8] {'lag'}, dimensions={1}, use_global_device_ids=true | all-gather | bytes 442368 | tf_op jit(solution)/shard_map/while/body/eval_jaxpr/all_gather | solution.py:84
  314.4 36.8 %reduce-scatter.5.cloned.1.call-done = f32[256,96]{0,1:T(8,128)} async-done(((f32[2048,96]{0,1:T(8,128)}), f32[256,96]{0,1:T(8,128)}) %reduce-scatter.5.cloned.1.call-update) | async-done | bytes 98320 | tf_op jit(solution)/shard_map/while/body/eval_jaxpr/reduce_scatter | solution.py:50
  352.2 17.5 %psum.25 = f32[96]{0:T(128)S(1)} all-reduce(f32[96]{0:T(128)S(1)} %broadcast_multiply_fusion.3), channel_id=1, replica_groups=mesh['blk'=32,'lag'=8] {'lag'}, use_global_device_ids=true, to_apply=%region_11.11 | all-reduce | flops 96 | bytes 768 | tf_op jit(solution)/shard_map/while/body/eval_jaxpr/psum | solution.py:80
  370.7 28.9 %all_gather.17 = bf16[96,2048]{1,0:T(8,128)(2,1)S(1)} all-gather(bf16[96,256]{1,0:T(8,128)(2,1)S(1)} %fusion.96), channel_id=1, replica_groups=mesh['blk'=32,'lag'=8] {'lag'}, dimensions={1}, use_global_device_ids=true | all-gather | bytes 442368 | tf_op jit(solution)/shard_map/while/body/eval_jaxpr/all_gather | solution.py:84
  411.9 36.6 %reduce-scatter.5.cloned.1.call-done = f32[256,96]{0,1:T(8,128)} async-done(((f32[2048,96]{0,1:T(8,128)}), f32[256,96]{0,1:T(8,128)}) %reduce-scatter.5.cloned.1.call-update) | async-done | bytes 98320 | tf_op jit(solution)/shard_map/while/body/eval_jaxpr/reduce_scatter | solution.py:50
  449.6 17.5 %psum.25 = f32[96]{0:T(128)S(1)} all-reduce(f32[96]{0:T(128)S(1)} %broadcast_multiply_fusion.3), channel_id=1, replica_groups=mesh['blk'=32,'lag'=8] {'lag'}, use_global_device_ids=true, to_apply=%region_11.11 | all-reduce | flops 96 | bytes 768 | tf_op jit(solution)/shard_map/while/body/eval_jaxpr/psum | solution.py:80
  468.1 28.8 %all_gather.17 = bf16[96,2048]{1,0:T(8,128)(2,1)S(1)} all-gather(bf16[96,256]{1,0:T(8,128)(2,1)S(1)} %fusion.96), channel_id=1, replica_groups=mesh['blk'=32,'lag'=8] {'lag'}, dimensions={1}, use_global_device_ids=true | all-gather | bytes 442368 | tf_op jit(solution)/shard_map/while/body/eval_jaxpr/all_gather | solution.py:84
  509.2 36.8 %reduce-scatter.5.cloned.1.call-done = f32[256,96]{0,1:T(8,128)} async-done(((f32[2048,96]{0,1:T(8,128)}), f32[256,96]{0,1:T(8,128)}) %reduce-scatter.5.cloned.1.call-update) | async-done | bytes 98320 | tf_op jit(solution)/shard_map/while/body/eval_jaxpr/reduce_scatter | solution.py:50
  565.5 28.8 %all_gather.17 = bf16[96,2048]{1,0:T(8,128)(2,1)S(1)} all-gather(bf16[96,256]{1,0:T(8,128)(2,1)S(1)} %fusion.96), channel_id=1, replica_groups=mesh['blk'=32,'lag'=8] {'lag'}, dimensions={1}, use_global_device_ids=true | all-gather | bytes 442368 | tf_op jit(solution)/shard_map/while/body/eval_jaxpr/all_gather | solution.py:84
  606.6 36.8 %reduce-scatter.5.cloned.1.call-done = f32[256,96]{0,1:T(8,128)} async-done(((f32[2048,96]{0,1:T(8,128)}), f32[256,96]{0,1:T(8,128)}) %reduce-scatter.5.cloned.1.call-update) | async-done | bytes 98320 | tf_op jit(solution)/shard_map/while/body/eval_jaxpr/reduce_scatter | solution.py:50
  644.4 17.5 %psum.25 = f32[96]{0:T(128)S(1)} all-reduce(f32[96]{0:T(128)S(1)} %broadcast_multiply_fusion.3), channel_id=1, replica_groups=mesh['blk'=32,'lag'=8] {'lag'}, use_global_device_ids=true, to_apply=%region_11.11 | all-reduce | flops 96 | bytes 768 | tf_op jit(solution)/shard_map/while/body/eval_jaxpr/psum | solution.py:80
  662.9 28.9 %all_gather.17 = bf16[96,2048]{1,0:T(8,128)(2,1)S(1)} all-gather(bf16[96,256]{1,0:T(8,128)(2,1)S(1)} %fusion.96), channel_id=1, replica_groups=mesh['blk'=32,'lag'=8] {'lag'}, dimensions={1}, use_global_device_ids=true | all-gather | bytes 442368 | tf_op jit(solution)/shard_map/while/body/eval_jaxpr/all_gather | solution.py:84
  704.1 36.7 %reduce-scatter.5.cloned.1.call-done = f32[256,96]{0,1:T(8,128)} async-done(((f32[2048,96]{0,1:T(8,128)}), f32[256,96]{0,1:T(8,128)}) %reduce-scatter.5.cloned.1.call-update) | async-done | bytes 98320 | tf_op jit(solution)/shard_map/while/body/eval_jaxpr/reduce_scatter | solution.py:50
  741.8 17.5 %psum.25 = f32[96]{0:T(128)S(1)} all-reduce(f32[96]{0:T(128)S(1)} %broadcast_multiply_fusion.3), channel_id=1, replica_groups=mesh['blk'=32,'lag'=8] {'lag'}, use_global_device_ids=true, to_apply=%region_11.11 | all-reduce | flops 96 | bytes 768 | tf_op jit(solution)/shard_map/while/body/eval_jaxpr/psum | solution.py:80
  760.3 28.9 %all_gather.17 = bf16[96,2048]{1,0:T(8,128)(2,1)S(1)} all-gather(bf16[96,256]{1,0:T(8,128)(2,1)S(1)} %fusion.96), channel_id=1, replica_groups=mesh['blk'=32,'lag'=8] {'lag'}, dimensions={1}, use_global_device_ids=true | all-gather | bytes 442368 | tf_op jit(solution)/shard_map/while/body/eval_jaxpr/all_gather | solution.py:84
  801.5 36.8 %reduce-scatter.5.cloned.1.call-done = f32[256,96]{0,1:T(8,128)} async-done(((f32[2048,96]{0,1:T(8,128)}), f32[256,96]{0,1:T(8,128)}) %reduce-scatter.5.cloned.1.call-update) | async-done | bytes 98320 | tf_op jit(solution)/shard_map/while/body/eval_jaxpr/reduce_scatter | solution.py:50
  857.7 28.9 %all_gather.17 = bf16[96,2048]{1,0:T(8,128)(2,1)S(1)} all-gather(bf16[96,256]{1,0:T(8,128)(2,1)S(1)} %fusion.96), channel_id=1, replica_groups=mesh['blk'=32,'lag'=8] {'lag'}, dimensions={1}, use_global_device_ids=true | all-gather | bytes 442368 | tf_op jit(solution)/shard_map/while/body/eval_jaxpr/all_gather | solution.py:84
  898.9 36.7 %reduce-scatter.5.cloned.1.call-done = f32[256,96]{0,1:T(8,128)} async-done(((f32[2048,96]{0,1:T(8,128)}), f32[256,96]{0,1:T(8,128)}) %reduce-scatter.5.cloned.1.call-update) | async-done | bytes 98320 | tf_op jit(solution)/shard_map/while/body/eval_jaxpr/reduce_scatter | solution.py:50
  936.6 17.5 %psum.25 = f32[96]{0:T(128)S(1)} all-reduce(f32[96]{0:T(128)S(1)} %broadcast_multiply_fusion.3), channel_id=1, replica_groups=mesh['blk'=32,'lag'=8] {'lag'}, use_global_device_ids=true, to_apply=%region_11.11 | all-reduce | flops 96 | bytes 768 | tf_op jit(solution)/shard_map/while/body/eval_jaxpr/psum | solution.py:80
  955.2 28.8 %all_gather.17 = bf16[96,2048]{1,0:T(8,128)(2,1)S(1)} all-gather(bf16[96,256]{1,0:T(8,128)(2,1)S(1)} %fusion.96), channel_id=1, replica_groups=mesh['blk'=32,'lag'=8] {'lag'}, dimensions={1}, use_global_device_ids=true | all-gather | bytes 442368 | tf_op jit(solution)/shard_map/while/body/eval_jaxpr/all_gather | solution.py:84
  996.3 36.7 %reduce-scatter.5.cloned.1.call-done = f32[256,96]{0,1:T(8,128)} async-done(((f32[2048,96]{0,1:T(8,128)}), f32[256,96]{0,1:T(8,128)}) %reduce-scatter.5.cloned.1.call-update) | async-done | bytes 98320 | tf_op jit(solution)/shard_map/while/body/eval_jaxpr/reduce_scatter | solution.py:50
  1034.0 17.6 %psum.25 = f32[96]{0:T(128)S(1)} all-reduce(f32[96]{0:T(128)S(1)} %broadcast_multiply_fusion.3), channel_id=1, replica_groups=mesh['blk'=32,'lag'=8] {'lag'}, use_global_device_ids=true, to_apply=%region_11.11 | all-reduce | flops 96 | bytes 768 | tf_op jit(solution)/shard_map/while/body/eval_jaxpr/psum | solution.py:80
  1052.6 28.8 %all_gather.17 = bf16[96,2048]{1,0:T(8,128)(2,1)S(1)} all-gather(bf16[96,256]{1,0:T(8,128)(2,1)S(1)} %fusion.96), channel_id=1, replica_groups=mesh['blk'=32,'lag'=8] {'lag'}, dimensions={1}, use_global_device_ids=true | all-gather | bytes 442368 | tf_op jit(solution)/shard_map/while/body/eval_jaxpr/all_gather | solution.py:84
  1093.6 36.8 %reduce-scatter.5.cloned.1.call-done = f32[256,96]{0,1:T(8,128)} async-done(((f32[2048,96]{0,1:T(8,128)}), f32[256,96]{0,1:T(8,128)}) %reduce-scatter.5.cloned.1.call-update) | async-done | bytes 98320 | tf_op jit(solution)/shard_map/while/body/eval_jaxpr/reduce_scatter | solution.py:50
  1131.4 17.5 %psum.25 = f32[96]{0:T(128)S(1)} all-reduce(f32[96]{0:T(128)S(1)} %broadcast_multiply_fusion.3), channel_id=1, replica_groups=mesh['blk'=32,'lag'=8] {'lag'}, use_global_device_ids=true, to_apply=%region_11.11 | all-reduce | flops 96 | bytes 768 | tf_op jit(solution)/shard_map/while/body/eval_jaxpr/psum | solution.py:80
  1149.9 28.9 %all_gather.17 = bf16[96,2048]{1,0:T(8,128)(2,1)S(1)} all-gather(bf16[96,256]{1,0:T(8,128)(2,1)S(1)} %fusion.96), channel_id=1, replica_groups=mesh['blk'=32,'lag'=8] {'lag'}, dimensions={1}, use_global_device_ids=true | all-gather | bytes 442368 | tf_op jit(solution)/shard_map/while/body/eval_jaxpr/all_gather | solution.py:84
  1191.1 36.7 %reduce-scatter.5.cloned.1.call-done = f32[256,96]{0,1:T(8,128)} async-done(((f32[2048,96]{0,1:T(8,128)}), f32[256,96]{0,1:T(8,128)}) %reduce-scatter.5.cloned.1.call-update) | async-done | bytes 98320 | tf_op jit(solution)/shard_map/while/body/eval_jaxpr/reduce_scatter | solution.py:50
  1228.8 17.5 %psum.25 = f32[96]{0:T(128)S(1)} all-reduce(f32[96]{0:T(128)S(1)} %broadcast_multiply_fusion.3), channel_id=1, replica_groups=mesh['blk'=32,'lag'=8] {'lag'}, use_global_device_ids=true, to_apply=%region_11.11 | all-reduce | flops 96 | bytes 768 | tf_op jit(solution)/shard_map/while/body/eval_jaxpr/psum | solution.py:80
  1247.3 28.8 %all_gather.17 = bf16[96,2048]{1,0:T(8,128)(2,1)S(1)} all-gather(bf16[96,256]{1,0:T(8,128)(2,1)S(1)} %fusion.96), channel_id=1, replica_groups=mesh['blk'=32,'lag'=8] {'lag'}, dimensions={1}, use_global_device_ids=true | all-gather | bytes 442368 | tf_op jit(solution)/shard_map/while/body/eval_jaxpr/all_gather | solution.py:84
  1288.5 36.8 %reduce-scatter.5.cloned.1.call-done = f32[256,96]{0,1:T(8,128)} async-done(((f32[2048,96]{0,1:T(8,128)}), f32[256,96]{0,1:T(8,128)}) %reduce-scatter.5.cloned.1.call-update) | async-done | bytes 98320 | tf_op jit(solution)/shard_map/while/body/eval_jaxpr/reduce_scatter | solution.py:50
  1344.7 28.9 %all_gather.17 = bf16[96,2048]{1,0:T(8,128)(2,1)S(1)} all-gather(bf16[96,256]{1,0:T(8,128)(2,1)S(1)} %fusion.96), channel_id=1, replica_groups=mesh['blk'=32,'lag'=8] {'lag'}, dimensions={1}, use_global_device_ids=true | all-gather | bytes 442368 | tf_op jit(solution)/shard_map/while/body/eval_jaxpr/all_gather | solution.py:84
  1385.9 36.7 %reduce-scatter.5.cloned.1.call-done = f32[256,96]{0,1:T(8,128)} async-done(((f32[2048,96]{0,1:T(8,128)}), f32[256,96]{0,1:T(8,128)}) %reduce-scatter.5.cloned.1.call-update) | async-done | bytes 98320 | tf_op jit(solution)/shard_map/while/body/eval_jaxpr/reduce_scatter | solution.py:50
  1423.6 17.5 %psum.25 = f32[96]{0:T(128)S(1)} all-reduce(f32[96]{0:T(128)S(1)} %broadcast_multiply_fusion.3), channel_id=1, replica_groups=mesh['blk'=32,'lag'=8] {'lag'}, use_global_device_ids=true, to_apply=%region_11.11 | all-reduce | flops 96 | bytes 768 | tf_op jit(solution)/shard_map/while/body/eval_jaxpr/psum | solution.py:80
  1442.1 28.9 %all_gather.17 = bf16[96,2048]{1,0:T(8,128)(2,1)S(1)} all-gather(bf16[96,256]{1,0:T(8,128)(2,1)S(1)} %fusion.96), channel_id=1, replica_groups=mesh['blk'=32,'lag'=8] {'lag'}, dimensions={1}, use_global_device_ids=true | all-gather | bytes 442368 | tf_op jit(solution)/shard_map/while/body/eval_jaxpr/all_gather | solution.py:84
  1483.3 36.7 %reduce-scatter.5.cloned.1.call-done = f32[256,96]{0,1:T(8,128)} async-done(((f32[2048,96]{0,1:T(8,128)}), f32[256,96]{0,1:T(8,128)}) %reduce-scatter.5.cloned.1.call-update) | async-done | bytes 98320 | tf_op jit(solution)/shard_map/while/body/eval_jaxpr/reduce_scatter | solution.py:50
  1521.0 17.5 %psum.25 = f32[96]{0:T(128)S(1)} all-reduce(f32[96]{0:T(128)S(1)} %broadcast_multiply_fusion.3), channel_id=1, replica_groups=mesh['blk'=32,'lag'=8] {'lag'}, use_global_device_ids=true, to_apply=%region_11.11 | all-reduce | flops 96 | bytes 768 | tf_op jit(solution)/shard_map/while/body/eval_jaxpr/psum | solution.py:80
  1539.5 28.8 %all_gather.17 = bf16[96,2048]{1,0:T(8,128)(2,1)S(1)} all-gather(bf16[96,256]{1,0:T(8,128)(2,1)S(1)} %fusion.96), channel_id=1, replica_groups=mesh['blk'=32,'lag'=8] {'lag'}, dimensions={1}, use_global_device_ids=true | all-gather | bytes 442368 | tf_op jit(solution)/shard_map/while/body/eval_jaxpr/all_gather | solution.py:84
  1580.7 36.8 %reduce-scatter.5.cloned.1.call-done = f32[256,96]{0,1:T(8,128)} async-done(((f32[2048,96]{0,1:T(8,128)}), f32[256,96]{0,1:T(8,128)}) %reduce-scatter.5.cloned.1.call-update) | async-done | bytes 98320 | tf_op jit(solution)/shard_map/while/body/eval_jaxpr/reduce_scatter | solution.py:50
  1618.5 17.5 %psum.25 = f32[96]{0:T(128)S(1)} all-reduce(f32[96]{0:T(128)S(1)} %broadcast_multiply_fusion.3), channel_id=1, replica_groups=mesh['blk'=32,'lag'=8] {'lag'}, use_global_device_ids=true, to_apply=%region_11.11 | all-reduce | flops 96 | bytes 768 | tf_op jit(solution)/shard_map/while/body/eval_jaxpr/psum | solution.py:80
  1637.0 28.9 %all_gather.17 = bf16[96,2048]{1,0:T(8,128)(2,1)S(1)} all-gather(bf16[96,256]{1,0:T(8,128)(2,1)S(1)} %fusion.96), channel_id=1, replica_groups=mesh['blk'=32,'lag'=8] {'lag'}, dimensions={1}, use_global_device_ids=true | all-gather | bytes 442368 | tf_op jit(solution)/shard_map/while/body/eval_jaxpr/all_gather | solution.py:84
  (540 shorter events, 319.7 us)
Async XLA Ops:
  6.5 52.4 %reduce-scatter.3.cloned.1.call-start = ((), (), s32[]{:S(2)}) async-start(), calls=%async_computation.2 | async-start | bytes 884736 | tf_op jit(solution)/shard_map/reduce_scatter | solution.py:50
  109.0 47.3 %reduce-scatter.5.cloned.1.call-start = ((), (), s32[]{:S(2)}) async-start(), calls=%async_computation.3 | async-start | bytes 884736 | tf_op jit(solution)/shard_map/while/body/eval_jaxpr/reduce_scatter | solution.py:50
  109.1 8.8 collective-permute-start
  119.4 86.7 %collective-permute-start.1 = (f32[128,768]{1,0:T(8,128)S(1)}, f32[128,768]{1,0:T(8,128)S(1)}, u32[]{:S(2)}, u32[]{:S(2)}) collective-permute-start(f32[128,768]{1,0:T(8,128)S(1)} %get-tuple-element.476), channel_id=1, source_target_pairs={{248,0},{0,8},{8,16},{16,24},{24,32},{32,40},{40,48},{48,56},{56,6... | collective-permute-start | bytes 1179656 | tf_op jit(solution)/shard_map/while/body/eval_jaxpr/ppermute | solution.py:11
  206.5 47.3 %reduce-scatter.5.cloned.1.call-start = ((), (), s32[]{:S(2)}) async-start(), calls=%async_computation.3 | async-start | bytes 884736 | tf_op jit(solution)/shard_map/while/body/eval_jaxpr/reduce_scatter | solution.py:50
  206.5 8.8 collective-permute-start
  216.9 86.5 %collective-permute-start.1 = (f32[128,768]{1,0:T(8,128)S(1)}, f32[128,768]{1,0:T(8,128)S(1)}, u32[]{:S(2)}, u32[]{:S(2)}) collective-permute-start(f32[128,768]{1,0:T(8,128)S(1)} %get-tuple-element.476), channel_id=1, source_target_pairs={{248,0},{0,8},{8,16},{16,24},{24,32},{32,40},{40,48},{48,56},{56,6... | collective-permute-start | bytes 1179656 | tf_op jit(solution)/shard_map/while/body/eval_jaxpr/ppermute | solution.py:11
  303.8 47.4 %reduce-scatter.5.cloned.1.call-start = ((), (), s32[]{:S(2)}) async-start(), calls=%async_computation.3 | async-start | bytes 884736 | tf_op jit(solution)/shard_map/while/body/eval_jaxpr/reduce_scatter | solution.py:50
  303.9 8.8 collective-permute-start
  314.3 86.7 %collective-permute-start.1 = (f32[128,768]{1,0:T(8,128)S(1)}, f32[128,768]{1,0:T(8,128)S(1)}, u32[]{:S(2)}, u32[]{:S(2)}) collective-permute-start(f32[128,768]{1,0:T(8,128)S(1)} %get-tuple-element.476), channel_id=1, source_target_pairs={{248,0},{0,8},{8,16},{16,24},{24,32},{32,40},{40,48},{48,56},{56,6... | collective-permute-start | bytes 1179656 | tf_op jit(solution)/shard_map/while/body/eval_jaxpr/ppermute | solution.py:11
  401.4 47.2 %reduce-scatter.5.cloned.1.call-start = ((), (), s32[]{:S(2)}) async-start(), calls=%async_computation.3 | async-start | bytes 884736 | tf_op jit(solution)/shard_map/while/body/eval_jaxpr/reduce_scatter | solution.py:50
  401.4 8.8 collective-permute-start
  411.8 86.5 %collective-permute-start.1 = (f32[128,768]{1,0:T(8,128)S(1)}, f32[128,768]{1,0:T(8,128)S(1)}, u32[]{:S(2)}, u32[]{:S(2)}) collective-permute-start(f32[128,768]{1,0:T(8,128)S(1)} %get-tuple-element.476), channel_id=1, source_target_pairs={{248,0},{0,8},{8,16},{16,24},{24,32},{32,40},{40,48},{48,56},{56,6... | collective-permute-start | bytes 1179656 | tf_op jit(solution)/shard_map/while/body/eval_jaxpr/ppermute | solution.py:11
  498.7 47.4 %reduce-scatter.5.cloned.1.call-start = ((), (), s32[]{:S(2)}) async-start(), calls=%async_computation.3 | async-start | bytes 884736 | tf_op jit(solution)/shard_map/while/body/eval_jaxpr/reduce_scatter | solution.py:50
  498.7 8.8 collective-permute-start
  509.1 86.6 %collective-permute-start.1 = (f32[128,768]{1,0:T(8,128)S(1)}, f32[128,768]{1,0:T(8,128)S(1)}, u32[]{:S(2)}, u32[]{:S(2)}) collective-permute-start(f32[128,768]{1,0:T(8,128)S(1)} %get-tuple-element.476), channel_id=1, source_target_pairs={{248,0},{0,8},{8,16},{16,24},{24,32},{32,40},{40,48},{48,56},{56,6... | collective-permute-start | bytes 1179656 | tf_op jit(solution)/shard_map/while/body/eval_jaxpr/ppermute | solution.py:11
  596.1 47.3 %reduce-scatter.5.cloned.1.call-start = ((), (), s32[]{:S(2)}) async-start(), calls=%async_computation.3 | async-start | bytes 884736 | tf_op jit(solution)/shard_map/while/body/eval_jaxpr/reduce_scatter | solution.py:50
  596.1 8.8 collective-permute-start
  606.5 86.6 %collective-permute-start.1 = (f32[128,768]{1,0:T(8,128)S(1)}, f32[128,768]{1,0:T(8,128)S(1)}, u32[]{:S(2)}, u32[]{:S(2)}) collective-permute-start(f32[128,768]{1,0:T(8,128)S(1)} %get-tuple-element.476), channel_id=1, source_target_pairs={{248,0},{0,8},{8,16},{16,24},{24,32},{32,40},{40,48},{48,56},{56,6... | collective-permute-start | bytes 1179656 | tf_op jit(solution)/shard_map/while/body/eval_jaxpr/ppermute | solution.py:11
  693.5 47.3 %reduce-scatter.5.cloned.1.call-start = ((), (), s32[]{:S(2)}) async-start(), calls=%async_computation.3 | async-start | bytes 884736 | tf_op jit(solution)/shard_map/while/body/eval_jaxpr/reduce_scatter | solution.py:50
  704.0 86.6 %collective-permute-start.1 = (f32[128,768]{1,0:T(8,128)S(1)}, f32[128,768]{1,0:T(8,128)S(1)}, u32[]{:S(2)}, u32[]{:S(2)}) collective-permute-start(f32[128,768]{1,0:T(8,128)S(1)} %get-tuple-element.476), channel_id=1, source_target_pairs={{248,0},{0,8},{8,16},{16,24},{24,32},{32,40},{40,48},{48,56},{56,6... | collective-permute-start | bytes 1179656 | tf_op jit(solution)/shard_map/while/body/eval_jaxpr/ppermute | solution.py:11
  790.9 47.3 %reduce-scatter.5.cloned.1.call-start = ((), (), s32[]{:S(2)}) async-start(), calls=%async_computation.3 | async-start | bytes 884736 | tf_op jit(solution)/shard_map/while/body/eval_jaxpr/reduce_scatter | solution.py:50
  791.0 8.8 collective-permute-start
  801.4 86.6 %collective-permute-start.1 = (f32[128,768]{1,0:T(8,128)S(1)}, f32[128,768]{1,0:T(8,128)S(1)}, u32[]{:S(2)}, u32[]{:S(2)}) collective-permute-start(f32[128,768]{1,0:T(8,128)S(1)} %get-tuple-element.476), channel_id=1, source_target_pairs={{248,0},{0,8},{8,16},{16,24},{24,32},{32,40},{40,48},{48,56},{56,6... | collective-permute-start | bytes 1179656 | tf_op jit(solution)/shard_map/while/body/eval_jaxpr/ppermute | solution.py:11
  888.4 47.2 %reduce-scatter.5.cloned.1.call-start = ((), (), s32[]{:S(2)}) async-start(), calls=%async_computation.3 | async-start | bytes 884736 | tf_op jit(solution)/shard_map/while/body/eval_jaxpr/reduce_scatter | solution.py:50
  888.4 8.8 collective-permute-start
  898.8 86.5 %collective-permute-start.1 = (f32[128,768]{1,0:T(8,128)S(1)}, f32[128,768]{1,0:T(8,128)S(1)}, u32[]{:S(2)}, u32[]{:S(2)}) collective-permute-start(f32[128,768]{1,0:T(8,128)S(1)} %get-tuple-element.476), channel_id=1, source_target_pairs={{248,0},{0,8},{8,16},{16,24},{24,32},{32,40},{40,48},{48,56},{56,6... | collective-permute-start | bytes 1179656 | tf_op jit(solution)/shard_map/while/body/eval_jaxpr/ppermute | solution.py:11
  985.7 47.3 %reduce-scatter.5.cloned.1.call-start = ((), (), s32[]{:S(2)}) async-start(), calls=%async_computation.3 | async-start | bytes 884736 | tf_op jit(solution)/shard_map/while/body/eval_jaxpr/reduce_scatter | solution.py:50
  985.8 8.8 collective-permute-start
  996.1 86.6 %collective-permute-start.1 = (f32[128,768]{1,0:T(8,128)S(1)}, f32[128,768]{1,0:T(8,128)S(1)}, u32[]{:S(2)}, u32[]{:S(2)}) collective-permute-start(f32[128,768]{1,0:T(8,128)S(1)} %get-tuple-element.476), channel_id=1, source_target_pairs={{248,0},{0,8},{8,16},{16,24},{24,32},{32,40},{40,48},{48,56},{56,6... | collective-permute-start | bytes 1179656 | tf_op jit(solution)/shard_map/while/body/eval_jaxpr/ppermute | solution.py:11
  1083.1 47.3 %reduce-scatter.5.cloned.1.call-start = ((), (), s32[]{:S(2)}) async-start(), calls=%async_computation.3 | async-start | bytes 884736 | tf_op jit(solution)/shard_map/while/body/eval_jaxpr/reduce_scatter | solution.py:50
  1093.5 86.6 %collective-permute-start.1 = (f32[128,768]{1,0:T(8,128)S(1)}, f32[128,768]{1,0:T(8,128)S(1)}, u32[]{:S(2)}, u32[]{:S(2)}) collective-permute-start(f32[128,768]{1,0:T(8,128)S(1)} %get-tuple-element.476), channel_id=1, source_target_pairs={{248,0},{0,8},{8,16},{16,24},{24,32},{32,40},{40,48},{48,56},{56,6... | collective-permute-start | bytes 1179656 | tf_op jit(solution)/shard_map/while/body/eval_jaxpr/ppermute | solution.py:11
  1180.5 47.3 %reduce-scatter.5.cloned.1.call-start = ((), (), s32[]{:S(2)}) async-start(), calls=%async_computation.3 | async-start | bytes 884736 | tf_op jit(solution)/shard_map/while/body/eval_jaxpr/reduce_scatter | solution.py:50
  1180.6 8.8 collective-permute-start
  1191.0 86.6 %collective-permute-start.1 = (f32[128,768]{1,0:T(8,128)S(1)}, f32[128,768]{1,0:T(8,128)S(1)}, u32[]{:S(2)}, u32[]{:S(2)}) collective-permute-start(f32[128,768]{1,0:T(8,128)S(1)} %get-tuple-element.476), channel_id=1, source_target_pairs={{248,0},{0,8},{8,16},{16,24},{24,32},{32,40},{40,48},{48,56},{56,6... | collective-permute-start | bytes 1179656 | tf_op jit(solution)/shard_map/while/body/eval_jaxpr/ppermute | solution.py:11
  1277.9 47.3 %reduce-scatter.5.cloned.1.call-start = ((), (), s32[]{:S(2)}) async-start(), calls=%async_computation.3 | async-start | bytes 884736 | tf_op jit(solution)/shard_map/while/body/eval_jaxpr/reduce_scatter | solution.py:50
  1278.0 8.8 collective-permute-start
  1288.3 86.6 %collective-permute-start.1 = (f32[128,768]{1,0:T(8,128)S(1)}, f32[128,768]{1,0:T(8,128)S(1)}, u32[]{:S(2)}, u32[]{:S(2)}) collective-permute-start(f32[128,768]{1,0:T(8,128)S(1)} %get-tuple-element.476), channel_id=1, source_target_pairs={{248,0},{0,8},{8,16},{16,24},{24,32},{32,40},{40,48},{48,56},{56,6... | collective-permute-start | bytes 1179656 | tf_op jit(solution)/shard_map/while/body/eval_jaxpr/ppermute | solution.py:11
  1375.3 47.3 %reduce-scatter.5.cloned.1.call-start = ((), (), s32[]{:S(2)}) async-start(), calls=%async_computation.3 | async-start | bytes 884736 | tf_op jit(solution)/shard_map/while/body/eval_jaxpr/reduce_scatter | solution.py:50
  1375.4 8.8 collective-permute-start
  1385.8 86.6 %collective-permute-start.1 = (f32[128,768]{1,0:T(8,128)S(1)}, f32[128,768]{1,0:T(8,128)S(1)}, u32[]{:S(2)}, u32[]{:S(2)}) collective-permute-start(f32[128,768]{1,0:T(8,128)S(1)} %get-tuple-element.476), channel_id=1, source_target_pairs={{248,0},{0,8},{8,16},{16,24},{24,32},{32,40},{40,48},{48,56},{56,6... | collective-permute-start | bytes 1179656 | tf_op jit(solution)/shard_map/while/body/eval_jaxpr/ppermute | solution.py:11
  1472.8 47.2 %reduce-scatter.5.cloned.1.call-start = ((), (), s32[]{:S(2)}) async-start(), calls=%async_computation.3 | async-start | bytes 884736 | tf_op jit(solution)/shard_map/while/body/eval_jaxpr/reduce_scatter | solution.py:50
  1472.8 8.8 collective-permute-start
  1483.2 86.5 %collective-permute-start.1 = (f32[128,768]{1,0:T(8,128)S(1)}, f32[128,768]{1,0:T(8,128)S(1)}, u32[]{:S(2)}, u32[]{:S(2)}) collective-permute-start(f32[128,768]{1,0:T(8,128)S(1)} %get-tuple-element.476), channel_id=1, source_target_pairs={{248,0},{0,8},{8,16},{16,24},{24,32},{32,40},{40,48},{48,56},{56,6... | collective-permute-start | bytes 1179656 | tf_op jit(solution)/shard_map/while/body/eval_jaxpr/ppermute | solution.py:11
  1570.1 47.3 %reduce-scatter.5.cloned.1.call-start = ((), (), s32[]{:S(2)}) async-start(), calls=%async_computation.3 | async-start | bytes 884736 | tf_op jit(solution)/shard_map/while/body/eval_jaxpr/reduce_scatter | solution.py:50
  1570.2 8.8 collective-permute-start
  1580.5 86.7 %collective-permute-start.1 = (f32[128,768]{1,0:T(8,128)S(1)}, f32[128,768]{1,0:T(8,128)S(1)}, u32[]{:S(2)}, u32[]{:S(2)}) collective-permute-start(f32[128,768]{1,0:T(8,128)S(1)} %get-tuple-element.476), channel_id=1, source_target_pairs={{248,0},{0,8},{8,16},{16,24},{24,32},{32,40},{40,48},{48,56},{56,6... | collective-permute-start | bytes 1179656 | tf_op jit(solution)/shard_map/while/body/eval_jaxpr/ppermute | solution.py:11
  1667.6 9.4 collective-permute-start.2
  (3 other events, 18.9 us)
Sparse Core Ops, SparseCore 0:
  16.2 42.7 reduce-scatter.2
  119.6 36.7 reduce-scatter.4
  217.0 36.6 reduce-scatter.4
  314.4 36.7 reduce-scatter.4
  411.9 36.5 reduce-scatter.4
  509.2 36.7 reduce-scatter.4
  606.6 36.7 reduce-scatter.4
  704.1 36.6 reduce-scatter.4
  801.5 36.7 reduce-scatter.4
  898.9 36.6 reduce-scatter.4
  996.3 36.6 reduce-scatter.4
  1093.6 36.7 reduce-scatter.4
  1191.1 36.6 reduce-scatter.4
  1288.5 36.7 reduce-scatter.4
  1385.9 36.6 reduce-scatter.4
  1483.3 36.6 reduce-scatter.4
  1580.7 36.7 reduce-scatter.4
where the time goes:
time: 1690 us; the launch traced here: 1680 us
  blocking collectives  788 us (47%)
  waiting for transfers between devices  743 us (44%)
  other arithmetic  53.9 us (3%)
  matrix products  48.1 us (3%)
  local copies, waits for them, and re-layouts  30.6 us (2%)
    reduce_scatter x17, waiting for transfers between devices, forward(): lax.psum_scatter(jnp.einsum('prf,rft->tp', cross, local_table, preferred_...  630 us
    all_gather x17, blocking collectives, correlate(): spectral = back(lax.all_gather(adjoint, 'lag', axis=1, tiled=True))  490 us
    psum x17, blocking collectives, correlate(): lax.psum(jnp.sum(weight[None, :] * lagged * lagged, axis=1) / lag_total,...  298 us
    ppermute x33, waiting for transfers between devices, from_behind(): return lax.ppermute(block, axis, route)  112 us
  transfers between devices with their start and end apart: 50, of which 34 were waited for; matrix products, arithmetic and copies ran while one was open for 5% of the time, Pallas kernels for 0%

commit v1 on v0

--- a/solution.py
+++ b/solution.py
@@ -81,7 +81,11 @@
         adjoint = (weight[None, :] * lagged / jnp.sqrt(energy + 1e-05)[:, None]).astype(
             jnp.bfloat16
         )
-        spectral = back(lax.all_gather(adjoint, "lag", axis=1, tiled=True))
+        spectral = back(
+            jnp.concatenate(
+                lax.all_to_all(jnp.stack([adjoint] * lax.axis_size("lag")), "lag", 0, 0), axis=1
+            )
+        )
         adj_real = spectral[:, None, 0]
         adj_imag = spectral[:, None, 1]
         near = jnp.stack(

time: 1690 us -> 1450 us (0.86)
  blocking collectives: 788 us -> 297 us
  waiting for transfers between devices: 743 us -> 878 us
  starting transfers between devices: 5.33 us -> 73.5 us
  local copies, waits for them, and re-layouts: 30.6 us -> 64.6 us
    all_gather x17 -> x0, blocking collectives: 490 us -> none  [correlate(): spectral = back(lax.all_gather(adjoint, 'lag', axis=1, tiled=True))]
    all_to_all x0 -> x17, waiting for transfers between devices: none -> 105 us  [correlate(): lax.all_to_all(jnp.stack([adjoint] * lax.axis_size('lag')), 'lag', 0, 0)]
    all_to_all x0 -> x17, starting transfers between devices: none -> 71.6 us  [correlate(): lax.all_to_all(jnp.stack([adjoint] * lax.axis_size('lag')), 'lag', 0, 0)]
    ppermute x33, waiting for transfers between devices: 112 us -> 165 us  [from_behind(): return lax.ppermute(block, axis, route)]
    reduce_scatter x17, waiting for transfers between devices: 630 us -> 608 us  [forward(): lax.psum_scatter(jnp.einsum('prf,rft->tp', cross, local_table, preferred_...]
  transfers between devices with their start and end apart: 50 -> 67, of which waited for: 34 -> 67; matrix products, arithmetic and copies ran while one was open for 5% -> 5% of each run, Pallas kernels for 0% -> 0%
where the time goes in v1:
time: 1450 us; the launch traced here: 1440 us
  waiting for transfers between devices  878 us (61%)
  blocking collectives  297 us (20%)
  starting transfers between devices  73.5 us (5%)
  local copies, waits for them, and re-layouts  64.6 us (4%)
  matrix products  60.3 us (4%)
  other arithmetic  54.4 us (4%)
    reduce_scatter x17, waiting for transfers between devices, forward(): lax.psum_scatter(jnp.einsum('prf,rft->tp', cross, local_table, preferred_...  608 us
    psum x17, blocking collectives, correlate(): lax.psum(jnp.sum(weight[None, :] * lagged * lagged, axis=1) / lag_total,...  297 us
    ppermute x33, waiting for transfers between devices, from_behind(): return lax.ppermute(block, axis, route)  165 us
    all_to_all x17, waiting for transfers between devices, correlate(): lax.all_to_all(jnp.stack([adjoint] * lax.axis_size('lag')), 'lag', 0, 0)  105 us
    all_to_all x17, starting transfers between devices, correlate(): lax.all_to_all(jnp.stack([adjoint] * lax.axis_size('lag')), 'lag', 0, 0)  71.6 us
  transfers between devices with their start and end apart: 67, of which 67 were waited for; matrix products, arithmetic and copies ran while one was open for 5% of the time, Pallas kernels for 0%

profile of v1, /device:TPU:8, one launch (start us, length us, event | category | flops | bytes accessed | tf_op | source)
XLA Modules:
  0.0 1443.8 jit_solution(8710925715459551032)
XLA Ops:
  16.1 42.9 %reduce-scatter.3.cloned.1.call-done = f32[256,96]{0,1:T(8,128)} async-done(((f32[2048,96]{0,1:T(8,128)}), f32[256,96]{0,1:T(8,128)}) %reduce-scatter.3.cloned.1.call-update) | async-done | bytes 98320 | tf_op jit(solution)/shard_map/reduce_scatter | solution.py:50
  60.0 17.5 %psum.21 = f32[96]{0:T(128)S(1)} all-reduce(f32[96]{0:T(128)S(1)} %broadcast_multiply_fusion.1), channel_id=1, replica_groups=mesh['blk'=32,'lag'=8] {'lag'}, use_global_device_ids=true, to_apply=%region_5.6 | all-reduce | flops 96 | bytes 768 | tf_op jit(solution)/shard_map/psum | solution.py:80
  94.6 1332.3 %while.21 = (s32[]{:T(128)}, bf16[128,3,2,128]{0,3,2,1:T(8,128)(2,1)S(1)}, f32[128,768]{1,0:T(8,128)S(1)}, f32[128,768]{1,0:T(8,128)}, s32[1,17,96,2]{2,3,1,0:T(...) while((s32[]{:T(128)}, ...), condition=%wide.region_12.13_spmd.clone.clone, body=%wide.region_6.12_spmd.clone.clone.sunk | while | flops 278300032 | bytes 19705452 | solution.py:121
  105.0 37.5 %reduce-scatter.5.cloned.1.call-done = f32[256,96]{0,1:T(8,128)} async-done(((f32[2048,96]{0,1:T(8,128)}), f32[256,96]{0,1:T(8,128)}) %reduce-scatter.5.cloned.1.call-update) | async-done | bytes 98320 | tf_op jit(solution)/shard_map/while/body/eval_jaxpr/reduce_scatter | solution.py:50
  143.5 17.5 %psum.25 = f32[96]{0:T(128)S(1)} all-reduce(f32[96]{0:T(128)S(1)} %broadcast_multiply_fusion.3), channel_id=1, replica_groups=mesh['blk'=32,'lag'=8] {'lag'}, use_global_device_ids=true, to_apply=%region_11.11 | all-reduce | flops 96 | bytes 768 | tf_op jit(solution)/shard_map/while/body/eval_jaxpr/psum | solution.py:80
  182.4 6.4 collective-permute-done
  190.5 35.1 %reduce-scatter.5.cloned.1.call-done = f32[256,96]{0,1:T(8,128)} async-done(((f32[2048,96]{0,1:T(8,128)}), f32[256,96]{0,1:T(8,128)}) %reduce-scatter.5.cloned.1.call-update) | async-done | bytes 98320 | tf_op jit(solution)/shard_map/while/body/eval_jaxpr/reduce_scatter | solution.py:50
  226.6 17.5 %psum.25 = f32[96]{0:T(128)S(1)} all-reduce(f32[96]{0:T(128)S(1)} %broadcast_multiply_fusion.3), channel_id=1, replica_groups=mesh['blk'=32,'lag'=8] {'lag'}, use_global_device_ids=true, to_apply=%region_11.11 | all-reduce | flops 96 | bytes 768 | tf_op jit(solution)/shard_map/while/body/eval_jaxpr/psum | solution.py:80
  265.5 6.4 collective-permute-done
  273.5 35.2 %reduce-scatter.5.cloned.1.call-done = f32[256,96]{0,1:T(8,128)} async-done(((f32[2048,96]{0,1:T(8,128)}), f32[256,96]{0,1:T(8,128)}) %reduce-scatter.5.cloned.1.call-update) | async-done | bytes 98320 | tf_op jit(solution)/shard_map/while/body/eval_jaxpr/reduce_scatter | solution.py:50
  309.7 17.5 %psum.25 = f32[96]{0:T(128)S(1)} all-reduce(f32[96]{0:T(128)S(1)} %broadcast_multiply_fusion.3), channel_id=1, replica_groups=mesh['blk'=32,'lag'=8] {'lag'}, use_global_device_ids=true, to_apply=%region_11.11 | all-reduce | flops 96 | bytes 768 | tf_op jit(solution)/shard_map/while/body/eval_jaxpr/psum | solution.py:80
  348.7 6.4 collective-permute-done
  356.7 35.1 %reduce-scatter.5.cloned.1.call-done = f32[256,96]{0,1:T(8,128)} async-done(((f32[2048,96]{0,1:T(8,128)}), f32[256,96]{0,1:T(8,128)}) %reduce-scatter.5.cloned.1.call-update) | async-done | bytes 98320 | tf_op jit(solution)/shard_map/while/body/eval_jaxpr/reduce_scatter | solution.py:50
  392.8 17.5 %psum.25 = f32[96]{0:T(128)S(1)} all-reduce(f32[96]{0:T(128)S(1)} %broadcast_multiply_fusion.3), channel_id=1, replica_groups=mesh['blk'=32,'lag'=8] {'lag'}, use_global_device_ids=true, to_apply=%region_11.11 | all-reduce | flops 96 | bytes 768 | tf_op jit(solution)/shard_map/while/body/eval_jaxpr/psum | solution.py:80
  431.8 6.4 collective-permute-done
  439.9 35.1 %reduce-scatter.5.cloned.1.call-done = f32[256,96]{0,1:T(8,128)} async-done(((f32[2048,96]{0,1:T(8,128)}), f32[256,96]{0,1:T(8,128)}) %reduce-scatter.5.cloned.1.call-update) | async-done | bytes 98320 | tf_op jit(solution)/shard_map/while/body/eval_jaxpr/reduce_scatter | solution.py:50
  475.9 17.5 %psum.25 = f32[96]{0:T(128)S(1)} all-reduce(f32[96]{0:T(128)S(1)} %broadcast_multiply_fusion.3), channel_id=1, replica_groups=mesh['blk'=32,'lag'=8] {'lag'}, use_global_device_ids=true, to_apply=%region_11.11 | all-reduce | flops 96 | bytes 768 | tf_op jit(solution)/shard_map/while/body/eval_jaxpr/psum | solution.py:80
  514.9 6.4 collective-permute-done
  522.9 35.2 %reduce-scatter.5.cloned.1.call-done = f32[256,96]{0,1:T(8,128)} async-done(((f32[2048,96]{0,1:T(8,128)}), f32[256,96]{0,1:T(8,128)}) %reduce-scatter.5.cloned.1.call-update) | async-done | bytes 98320 | tf_op jit(solution)/shard_map/while/body/eval_jaxpr/reduce_scatter | solution.py:50
  559.1 17.4 %psum.25 = f32[96]{0:T(128)S(1)} all-reduce(f32[96]{0:T(128)S(1)} %broadcast_multiply_fusion.3), channel_id=1, replica_groups=mesh['blk'=32,'lag'=8] {'lag'}, use_global_device_ids=true, to_apply=%region_11.11 | all-reduce | flops 96 | bytes 768 | tf_op jit(solution)/shard_map/while/body/eval_jaxpr/psum | solution.py:80
  598.0 6.4 collective-permute-done
  606.0 35.2 %reduce-scatter.5.cloned.1.call-done = f32[256,96]{0,1:T(8,128)} async-done(((f32[2048,96]{0,1:T(8,128)}), f32[256,96]{0,1:T(8,128)}) %reduce-scatter.5.cloned.1.call-update) | async-done | bytes 98320 | tf_op jit(solution)/shard_map/while/body/eval_jaxpr/reduce_scatter | solution.py:50
  642.2 17.4 %psum.25 = f32[96]{0:T(128)S(1)} all-reduce(f32[96]{0:T(128)S(1)} %broadcast_multiply_fusion.3), channel_id=1, replica_groups=mesh['blk'=32,'lag'=8] {'lag'}, use_global_device_ids=true, to_apply=%region_11.11 | all-reduce | flops 96 | bytes 768 | tf_op jit(solution)/shard_map/while/body/eval_jaxpr/psum | solution.py:80
  681.1 6.4 collective-permute-done
  689.1 35.2 %reduce-scatter.5.cloned.1.call-done = f32[256,96]{0,1:T(8,128)} async-done(((f32[2048,96]{0,1:T(8,128)}), f32[256,96]{0,1:T(8,128)}) %reduce-scatter.5.cloned.1.call-update) | async-done | bytes 98320 | tf_op jit(solution)/shard_map/while/body/eval_jaxpr/reduce_scatter | solution.py:50
  725.3 17.5 %psum.25 = f32[96]{0:T(128)S(1)} all-reduce(f32[96]{0:T(128)S(1)} %broadcast_multiply_fusion.3), channel_id=1, replica_groups=mesh['blk'=32,'lag'=8] {'lag'}, use_global_device_ids=true, to_apply=%region_11.11 | all-reduce | flops 96 | bytes 768 | tf_op jit(solution)/shard_map/while/body/eval_jaxpr/psum | solution.py:80
  764.3 6.4 collective-permute-done
  772.3 35.2 %reduce-scatter.5.cloned.1.call-done = f32[256,96]{0,1:T(8,128)} async-done(((f32[2048,96]{0,1:T(8,128)}), f32[256,96]{0,1:T(8,128)}) %reduce-scatter.5.cloned.1.call-update) | async-done | bytes 98320 | tf_op jit(solution)/shard_map/while/body/eval_jaxpr/reduce_scatter | solution.py:50
  808.5 17.4 %psum.25 = f32[96]{0:T(128)S(1)} all-reduce(f32[96]{0:T(128)S(1)} %broadcast_multiply_fusion.3), channel_id=1, replica_groups=mesh['blk'=32,'lag'=8] {'lag'}, use_global_device_ids=true, to_apply=%region_11.11 | all-reduce | flops 96 | bytes 768 | tf_op jit(solution)/shard_map/while/body/eval_jaxpr/psum | solution.py:80
  847.3 6.4 collective-permute-done
  855.4 35.2 %reduce-scatter.5.cloned.1.call-done = f32[256,96]{0,1:T(8,128)} async-done(((f32[2048,96]{0,1:T(8,128)}), f32[256,96]{0,1:T(8,128)}) %reduce-scatter.5.cloned.1.call-update) | async-done | bytes 98320 | tf_op jit(solution)/shard_map/while/body/eval_jaxpr/reduce_scatter | solution.py:50
  891.6 17.4 %psum.25 = f32[96]{0:T(128)S(1)} all-reduce(f32[96]{0:T(128)S(1)} %broadcast_multiply_fusion.3), channel_id=1, replica_groups=mesh['blk'=32,'lag'=8] {'lag'}, use_global_device_ids=true, to_apply=%region_11.11 | all-reduce | flops 96 | bytes 768 | tf_op jit(solution)/shard_map/while/body/eval_jaxpr/psum | solution.py:80
  930.4 6.4 collective-permute-done
  938.4 35.2 %reduce-scatter.5.cloned.1.call-done = f32[256,96]{0,1:T(8,128)} async-done(((f32[2048,96]{0,1:T(8,128)}), f32[256,96]{0,1:T(8,128)}) %reduce-scatter.5.cloned.1.call-update) | async-done | bytes 98320 | tf_op jit(solution)/shard_map/while/body/eval_jaxpr/reduce_scatter | solution.py:50
  974.7 17.5 %psum.25 = f32[96]{0:T(128)S(1)} all-reduce(f32[96]{0:T(128)S(1)} %broadcast_multiply_fusion.3), channel_id=1, replica_groups=mesh['blk'=32,'lag'=8] {'lag'}, use_global_device_ids=true, to_apply=%region_11.11 | all-reduce | flops 96 | bytes 768 | tf_op jit(solution)/shard_map/while/body/eval_jaxpr/psum | solution.py:80
  1021.6 35.2 %reduce-scatter.5.cloned.1.call-done = f32[256,96]{0,1:T(8,128)} async-done(((f32[2048,96]{0,1:T(8,128)}), f32[256,96]{0,1:T(8,128)}) %reduce-scatter.5.cloned.1.call-update) | async-done | bytes 98320 | tf_op jit(solution)/shard_map/while/body/eval_jaxpr/reduce_scatter | solution.py:50
  1057.8 17.4 %psum.25 = f32[96]{0:T(128)S(1)} all-reduce(f32[96]{0:T(128)S(1)} %broadcast_multiply_fusion.3), channel_id=1, replica_groups=mesh['blk'=32,'lag'=8] {'lag'}, use_global_device_ids=true, to_apply=%region_11.11 | all-reduce | flops 96 | bytes 768 | tf_op jit(solution)/shard_map/while/body/eval_jaxpr/psum | solution.py:80
  1104.6 35.2 %reduce-scatter.5.cloned.1.call-done = f32[256,96]{0,1:T(8,128)} async-done(((f32[2048,96]{0,1:T(8,128)}), f32[256,96]{0,1:T(8,128)}) %reduce-scatter.5.cloned.1.call-update) | async-done | bytes 98320 | tf_op jit(solution)/shard_map/while/body/eval_jaxpr/reduce_scatter | solution.py:50
  1140.9 17.5 %psum.25 = f32[96]{0:T(128)S(1)} all-reduce(f32[96]{0:T(128)S(1)} %broadcast_multiply_fusion.3), channel_id=1, replica_groups=mesh['blk'=32,'lag'=8] {'lag'}, use_global_device_ids=true, to_apply=%region_11.11 | all-reduce | flops 96 | bytes 768 | tf_op jit(solution)/shard_map/while/body/eval_jaxpr/psum | solution.py:80
  1179.7 6.4 collective-permute-done
  1187.7 35.2 %reduce-scatter.5.cloned.1.call-done = f32[256,96]{0,1:T(8,128)} async-done(((f32[2048,96]{0,1:T(8,128)}), f32[256,96]{0,1:T(8,128)}) %reduce-scatter.5.cloned.1.call-update) | async-done | bytes 98320 | tf_op jit(solution)/shard_map/while/body/eval_jaxpr/reduce_scatter | solution.py:50
  1224.0 17.4 %psum.25 = f32[96]{0:T(128)S(1)} all-reduce(f32[96]{0:T(128)S(1)} %broadcast_multiply_fusion.3), channel_id=1, replica_groups=mesh['blk'=32,'lag'=8] {'lag'}, use_global_device_ids=true, to_apply=%region_11.11 | all-reduce | flops 96 | bytes 768 | tf_op jit(solution)/shard_map/while/body/eval_jaxpr/psum | solution.py:80
  1262.9 6.4 collective-permute-done
  1270.9 35.2 %reduce-scatter.5.cloned.1.call-done = f32[256,96]{0,1:T(8,128)} async-done(((f32[2048,96]{0,1:T(8,128)}), f32[256,96]{0,1:T(8,128)}) %reduce-scatter.5.cloned.1.call-update) | async-done | bytes 98320 | tf_op jit(solution)/shard_map/while/body/eval_jaxpr/reduce_scatter | solution.py:50
  1307.1 17.5 %psum.25 = f32[96]{0:T(128)S(1)} all-reduce(f32[96]{0:T(128)S(1)} %broadcast_multiply_fusion.3), channel_id=1, replica_groups=mesh['blk'=32,'lag'=8] {'lag'}, use_global_device_ids=true, to_apply=%region_11.11 | all-reduce | flops 96 | bytes 768 | tf_op jit(solution)/shard_map/while/body/eval_jaxpr/psum | solution.py:80
  1354.0 35.2 %reduce-scatter.5.cloned.1.call-done = f32[256,96]{0,1:T(8,128)} async-done(((f32[2048,96]{0,1:T(8,128)}), f32[256,96]{0,1:T(8,128)}) %reduce-scatter.5.cloned.1.call-update) | async-done | bytes 98320 | tf_op jit(solution)/shard_map/while/body/eval_jaxpr/reduce_scatter | solution.py:50
  1390.2 17.5 %psum.25 = f32[96]{0:T(128)S(1)} all-reduce(f32[96]{0:T(128)S(1)} %broadcast_multiply_fusion.3), channel_id=1, replica_groups=mesh['blk'=32,'lag'=8] {'lag'}, use_global_device_ids=true, to_apply=%region_11.11 | all-reduce | flops 96 | bytes 768 | tf_op jit(solution)/shard_map/while/body/eval_jaxpr/psum | solution.py:80
  1428.4 7.9 collective-permute-done.2
  (642 shorter events, 438.1 us)
Async XLA Ops:
  6.5 52.4 %reduce-scatter.3.cloned.1.call-start = ((), (), s32[]{:S(2)}) async-start(), calls=%async_computation.4 | async-start | bytes 884736 | tf_op jit(solution)/shard_map/reduce_scatter | solution.py:50
  94.6 47.9 %reduce-scatter.5.cloned.1.call-start = ((), (), s32[]{:S(2)}) async-start(), calls=%async_computation.5 | async-start | bytes 884736 | tf_op jit(solution)/shard_map/while/body/eval_jaxpr/reduce_scatter | solution.py:50
  162.8 11.1 all-to-all-start
  167.0 12.1 collective-permute-start.1
  180.1 45.4 %reduce-scatter.5.cloned.1.call-start = ((), (), s32[]{:S(2)}) async-start(), calls=%async_computation.5 | async-start | bytes 884736 | tf_op jit(solution)/shard_map/while/body/eval_jaxpr/reduce_scatter | solution.py:50
  245.8 11.0 all-to-all-start
  250.0 12.1 collective-permute-start.1
  263.2 45.5 %reduce-scatter.5.cloned.1.call-start = ((), (), s32[]{:S(2)}) async-start(), calls=%async_computation.5 | async-start | bytes 884736 | tf_op jit(solution)/shard_map/while/body/eval_jaxpr/reduce_scatter | solution.py:50
  329.0 11.1 all-to-all-start
  333.2 12.1 collective-permute-start.1
  346.4 45.4 %reduce-scatter.5.cloned.1.call-start = ((), (), s32[]{:S(2)}) async-start(), calls=%async_computation.5 | async-start | bytes 884736 | tf_op jit(solution)/shard_map/while/body/eval_jaxpr/reduce_scatter | solution.py:50
  412.1 11.3 all-to-all-start
  416.4 12.0 collective-permute-start.1
  429.5 45.4 %reduce-scatter.5.cloned.1.call-start = ((), (), s32[]{:S(2)}) async-start(), calls=%async_computation.5 | async-start | bytes 884736 | tf_op jit(solution)/shard_map/while/body/eval_jaxpr/reduce_scatter | solution.py:50
  495.2 11.0 all-to-all-start
  499.4 12.1 collective-permute-start.1
  512.6 45.5 %reduce-scatter.5.cloned.1.call-start = ((), (), s32[]{:S(2)}) async-start(), calls=%async_computation.5 | async-start | bytes 884736 | tf_op jit(solution)/shard_map/while/body/eval_jaxpr/reduce_scatter | solution.py:50
  578.3 11.1 all-to-all-start
  582.5 12.1 collective-permute-start.1
  595.7 45.5 %reduce-scatter.5.cloned.1.call-start = ((), (), s32[]{:S(2)}) async-start(), calls=%async_computation.5 | async-start | bytes 884736 | tf_op jit(solution)/shard_map/while/body/eval_jaxpr/reduce_scatter | solution.py:50
  661.4 11.1 all-to-all-start
  665.6 12.1 collective-permute-start.1
  678.8 45.5 %reduce-scatter.5.cloned.1.call-start = ((), (), s32[]{:S(2)}) async-start(), calls=%async_computation.5 | async-start | bytes 884736 | tf_op jit(solution)/shard_map/while/body/eval_jaxpr/reduce_scatter | solution.py:50
  744.6 11.1 all-to-all-start
  748.8 12.1 collective-permute-start.1
  762.0 45.5 %reduce-scatter.5.cloned.1.call-start = ((), (), s32[]{:S(2)}) async-start(), calls=%async_computation.5 | async-start | bytes 884736 | tf_op jit(solution)/shard_map/while/body/eval_jaxpr/reduce_scatter | solution.py:50
  827.7 11.1 all-to-all-start
  831.9 12.1 collective-permute-start.1
  845.0 45.5 %reduce-scatter.5.cloned.1.call-start = ((), (), s32[]{:S(2)}) async-start(), calls=%async_computation.5 | async-start | bytes 884736 | tf_op jit(solution)/shard_map/while/body/eval_jaxpr/reduce_scatter | solution.py:50
  910.8 11.0 all-to-all-start
  915.0 12.1 collective-permute-start.1
  928.1 45.5 %reduce-scatter.5.cloned.1.call-start = ((), (), s32[]{:S(2)}) async-start(), calls=%async_computation.5 | async-start | bytes 884736 | tf_op jit(solution)/shard_map/while/body/eval_jaxpr/reduce_scatter | solution.py:50
  993.9 11.1 all-to-all-start
  998.1 12.1 collective-permute-start.1
  1011.3 45.5 %reduce-scatter.5.cloned.1.call-start = ((), (), s32[]{:S(2)}) async-start(), calls=%async_computation.5 | async-start | bytes 884736 | tf_op jit(solution)/shard_map/while/body/eval_jaxpr/reduce_scatter | solution.py:50
  1077.0 11.0 all-to-all-start
  1081.2 12.1 collective-permute-start.1
  1094.3 45.5 %reduce-scatter.5.cloned.1.call-start = ((), (), s32[]{:S(2)}) async-start(), calls=%async_computation.5 | async-start | bytes 884736 | tf_op jit(solution)/shard_map/while/body/eval_jaxpr/reduce_scatter | solution.py:50
  1164.3 12.1 collective-permute-start.1
  1177.4 45.5 %reduce-scatter.5.cloned.1.call-start = ((), (), s32[]{:S(2)}) async-start(), calls=%async_computation.5 | async-start | bytes 884736 | tf_op jit(solution)/shard_map/while/body/eval_jaxpr/reduce_scatter | solution.py:50
  1243.2 11.1 all-to-all-start
  1247.4 12.1 collective-permute-start.1
  1260.6 45.5 %reduce-scatter.5.cloned.1.call-start = ((), (), s32[]{:S(2)}) async-start(), calls=%async_computation.5 | async-start | bytes 884736 | tf_op jit(solution)/shard_map/while/body/eval_jaxpr/reduce_scatter | solution.py:50
  1326.3 11.1 all-to-all-start
  1330.5 12.1 collective-permute-start.1
  1343.7 45.5 %reduce-scatter.5.cloned.1.call-start = ((), (), s32[]{:S(2)}) async-start(), calls=%async_computation.5 | async-start | bytes 884736 | tf_op jit(solution)/shard_map/while/body/eval_jaxpr/reduce_scatter | solution.py:50
  1409.4 11.1 all-to-all-start
  1413.7 12.1 collective-permute-start.1
  (37 other events, 252.7 us)
Sparse Core Ops, SparseCore 0:
  16.2 42.7 reduce-scatter.2
  105.1 37.3 reduce-scatter.4
  190.6 34.9 reduce-scatter.4
  273.6 35.0 reduce-scatter.4
  356.8 34.9 reduce-scatter.4
  440.0 34.9 reduce-scatter.4
  523.0 35.0 reduce-scatter.4
  606.1 35.0 reduce-scatter.4
  689.2 35.0 reduce-scatter.4
  772.4 35.0 reduce-scatter.4
  855.5 35.0 reduce-scatter.4
  938.5 35.0 reduce-scatter.4
  1021.7 35.0 reduce-scatter.4
  1104.7 35.0 reduce-scatter.4
  1187.8 35.0 reduce-scatter.4
  1271.0 35.0 reduce-scatter.4
  1354.1 35.0 reduce-scatter.4
